TPU v7x, 128 devices: a whole 4x4x4 slice. The times are simulated.
128 devices in a mesh: chan: 32 (over z_lo, y, x), seg: 4 (over z_hi, core).
Axes of the slice: x: 4, y: 4, z: 4 (z_hi: 2, z_lo: 2; z = z_hi * 2 + z_lo), core: 2. Of those that a mesh axis runs over, the one named last changes fastest.
Arguments:
- traces: bfloat16 [4096, 8, 8192], P('chan', 'seg'), may hold values from -20 to 20
- pair_offsets: int32 [32, 16], replicated, may hold values from 1 to 31, as said below
- pair_counts: int32 [32], replicated, may hold values from 1 to 16, 64 in all
- pair_owner: int32 [64], replicated, may hold values from 0 to 63, each once
Outputs:
- correlations: float32 [128, 64, 128, 256], P('seg', 'chan')
Inputs may be any that keep to these rules, and one draw needn't show every extreme that they name: `pair_offsets`: row a lists 16 distinct offsets; only its first pair_counts[a] entries name pairs. `pair_counts`: the counts sum to 64. `pair_owner`: every slot number appears once.
All inputs are finite; a program needn't handle non-finite values.
Results may differ from a plain program's by a relative error of at most 0.017.
Values may be sent and summed in bfloat16 or wider, within the bound.
No kernel may reach another device: no remote copies, remote signals or barrier semaphores. Data moves between devices by JAX's collectives and lax.ppermute only.
A program may use at most 128 MiB of HBM per device.

v0:
```python
import math
import jax
import jax.numpy as jnp
from jax import lax
from jax.sharding import PartitionSpec as P

SAMPLES = 8192
BAND_START = 32
FREQS = 512
HALF = 8
LAGS = 256
TILE_DEV = 2


def smoother(bin_count):
    bins_axis = lax.iota(jnp.int32, bin_count)
    nearby = (jnp.abs(bins_axis[:, None] - bins_axis[None, :]) <= HALF).astype(jnp.float32)
    return nearby / jnp.sum(nearby, axis=0, keepdims=True)


def lag_table(first_bin, bin_count):
    bins_axis = BAND_START + first_bin + lax.iota(jnp.int32, bin_count)
    shifts = jnp.mod(lax.iota(jnp.int32, LAGS) - LAGS // 2, SAMPLES)
    phase_index = jnp.mod(bins_axis[:, None] * shifts[None, :], SAMPLES)
    angles = phase_index.astype(jnp.float32) * (2.0 * math.pi / SAMPLES)
    return jnp.concatenate([jnp.cos(angles), -jnp.sin(angles)], axis=0).astype(jnp.bfloat16)


def pair_blocks(pair_offsets, pair_counts, pair_owner, block_count, slot_count):
    slot_index = lax.iota(jnp.int32, slot_count)
    starts = jnp.cumsum(pair_counts) - pair_counts
    first_block = jnp.sum((starts[None, :] <= slot_index[:, None]).astype(jnp.int32), axis=1) - 1
    member = lax.iota(jnp.int32, block_count)[None, :] == first_block[:, None]
    start_of = jnp.sum(jnp.where(member, starts[None, :], 0), axis=1)
    position = slot_index - start_of
    listed = jnp.sum(jnp.where(member[:, :, None], pair_offsets[None, :, :], 0), axis=1)
    chosen = lax.iota(jnp.int32, pair_offsets.shape[1])[None, :] == position[:, None]
    offset = jnp.sum(jnp.where(chosen, listed, 0), axis=1)
    second_block = jnp.mod(first_block + offset, block_count)
    held = pair_owner[None, :] == slot_index[:, None]
    slot_first = jnp.sum(jnp.where(held, first_block[None, :], 0), axis=1)
    slot_second = jnp.sum(jnp.where(held, second_block[None, :], 0), axis=1)
    return (slot_first, slot_second)


def cross_terms(first_spec, second_spec):
    turned = jnp.stack([first_spec[:, :, :, 1], -first_spec[:, :, :, 0]], axis=3)
    real_part = jnp.einsum(
        "tispf,tjspf->itjf", first_spec, second_spec, preferred_element_type=jnp.float32
    )
    imag_part = jnp.einsum(
        "tispf,tjspf->itjf", turned, second_spec, preferred_element_type=jnp.float32
    )
    return jnp.stack([real_part, imag_part], axis=3).astype(jnp.bfloat16)


def invert(spectra, table, norm_factor):
    flat = spectra.reshape(-1, spectra.shape[3] * spectra.shape[4])
    lagged = jnp.dot(flat, table, preferred_element_type=jnp.float32) * norm_factor
    return lagged.reshape(spectra.shape[:3] + (table.shape[1],))


def on_device(traces, pair_offsets, pair_counts, pair_owner):
    block_size, local_segs, sample_count = traces.shape
    parts_count = lax.axis_size("seg")
    block_count = lax.axis_size("chan")
    quarter_bins = FREQS // parts_count
    all_segs = local_segs * parts_count
    norm_factor = 1.0 / math.sqrt(FREQS * all_segs)
    signal = traces.reshape(block_size * local_segs, sample_count)
    width_bins = min(128, FREQS)
    pieces_count = FREQS // width_bins
    times_axis = lax.iota(jnp.int32, sample_count)

    def transform(piece_index):
        bins_axis = BAND_START + piece_index * width_bins + lax.iota(jnp.int32, width_bins)
        phase_index = jnp.mod(times_axis[:, None] * bins_axis[None, :], sample_count)
        angles = phase_index.astype(jnp.float32) * (2.0 * math.pi / sample_count)
        table_part = jnp.concatenate([jnp.cos(angles), -jnp.sin(angles)], axis=1)
        table_high = table_part.astype(jnp.bfloat16)
        table_low = (table_part - table_high.astype(jnp.float32)).astype(jnp.bfloat16)
        upper = jnp.dot(signal, table_high, preferred_element_type=jnp.float32)
        return upper + jnp.dot(signal, table_low, preferred_element_type=jnp.float32)

    spectrum = lax.map(transform, lax.iota(jnp.int32, pieces_count))
    spectrum = (
        spectrum.reshape(pieces_count, -1, 2, width_bins)
        .transpose(1, 2, 0, 3)
        .reshape(-1, 2, FREQS)
    )
    real_part = spectrum[:, 0]
    imag_part = spectrum[:, 1]
    amplitude = jnp.sqrt(real_part * real_part + imag_part * imag_part)
    smoothed = jnp.dot(
        amplitude,
        smoother(FREQS),
        precision=lax.Precision.HIGHEST,
        preferred_element_type=jnp.float32,
    )
    divisor = jnp.maximum(smoothed, 1.0)
    whitened = jnp.stack([real_part / divisor, imag_part / divisor], axis=1).astype(jnp.bfloat16)
    whitened = whitened.reshape(block_size, local_segs, 2, parts_count, quarter_bins)
    quarter = lax.all_to_all(whitened, "seg", split_axis=3, concat_axis=1, tiled=True)
    quarter = quarter.reshape(block_size, all_segs, 2, quarter_bins)
    slot_first, slot_second = pair_blocks(
        pair_offsets, pair_counts, pair_owner, block_count, TILE_DEV * block_count
    )
    my_start = lax.axis_index("chan") * TILE_DEV
    needed = jnp.concatenate(
        [
            lax.dynamic_slice_in_dim(slot_first, my_start, TILE_DEV),
            lax.dynamic_slice_in_dim(slot_second, my_start, TILE_DEV),
        ]
    )
    empty_blocks = jnp.zeros((2 * TILE_DEV, block_size, all_segs, 2, quarter_bins), jnp.bfloat16)
    incoming = lax.all_gather(quarter, "chan", axis=0, tiled=True)
    block_total = incoming.shape[0] // block_size
    incoming_blocks = incoming.reshape(block_total, block_size, all_segs, 2, quarter_bins)
    inside = (needed >= 0) & (needed < block_total)
    picked = jnp.take(incoming_blocks, jnp.clip(needed, 0, block_total - 1), axis=0)
    held_blocks = jnp.where(inside[:, None, None, None, None], picked, empty_blocks)
    first_spec = held_blocks[:TILE_DEV]
    second_spec = held_blocks[TILE_DEV:]
    full_table = lag_table(0, FREQS)
    spectra = cross_terms(first_spec, second_spec)
    return invert(
        lax.all_to_all(spectra, "seg", split_axis=0, concat_axis=4, tiled=True),
        full_table,
        norm_factor,
    )


def solution(mesh):
    placed = (P("chan", "seg", None), P(), P(), P())
    return jax.shard_map(
        on_device,
        mesh=mesh,
        in_specs=placed,
        out_specs=P("seg", "chan", None, None),
        check_vma=False,
    )
```

profile of v0, /device:TPU:1, one launch (start us, length us, event | category | flops | bytes accessed | tf_op | source)
XLA Modules:
  0.0 643.9 jit_solution(6079321119400441198)
XLA Ops:
  6.6 7.2 %reshape.215 = bf16[256,8192]{1,0:T(8,128)(2,1)} reshape(bf16[128,2,8192]{2,1,0:T(2,128)(2,1)} %param.6) | data formatting | bytes 8388608 | tf_op jit(solution)/shard_map/reshape | solution.py:70
  13.8 82.4 %while.13 = (s32[]{:T(128)}, f32[4,256,256]{1,2,0:T(8,128)S(1)}, s32[4]{0:T(128)S(1)}, bf16[256,8192]{1,0:T(8,128)(2,1)}, s32[]{:T(128)}, /*index=5*/s32[1]{0:T(128)}, s32[1]{0:T(128)}) while((s32[]{:T(128)}, f32[4,256,256]{1,2,0:T(8,128)S(1)}, s32[4]{0:T(128)S(1)}, bf16[256,8192]{1,0:T(8,128)(2,1)}, s32[]{:T(128)}, ...), condition=%wide.region_8.9_spmd.clone, body=%wide.region_7.8_spmd.clone.sunk | while | flops 2182152192 | bytes 51119252 | solution.py:85
  15.2 16.5 %fusion.57 = (f32[8192,128]{1,0:T(8,128)S(1)}, f32[8192,128]{1,0:T(8,128)S(1)}) fusion(s32[128]{0:T(128)S(1)} %iota_add_fusion.3), kind=kLoop, calls=%fused_computation.18.clone.1 | loop fusion | flops 15728640 | bytes 8389120 | tf_op jit(solution)/shard_map/while/body/eval_jaxpr/cos | solution.py:79
  31.7 1.3 fusion.58
  33.0 1.3 fusion.59
  34.4 0.7 dynamic_slice.19
  35.7 16.5 %fusion.57 = (f32[8192,128]{1,0:T(8,128)S(1)}, f32[8192,128]{1,0:T(8,128)S(1)}) fusion(s32[128]{0:T(128)S(1)} %iota_add_fusion.3), kind=kLoop, calls=%fused_computation.18.clone.1 | loop fusion | flops 15728640 | bytes 8389120 | tf_op jit(solution)/shard_map/while/body/eval_jaxpr/cos | solution.py:79
  52.3 1.3 fusion.58
  53.6 1.3 fusion.59
  54.9 0.7 dynamic_slice.19
  56.3 16.5 %fusion.57 = (f32[8192,128]{1,0:T(8,128)S(1)}, f32[8192,128]{1,0:T(8,128)S(1)}) fusion(s32[128]{0:T(128)S(1)} %iota_add_fusion.3), kind=kLoop, calls=%fused_computation.18.clone.1 | loop fusion | flops 15728640 | bytes 8389120 | tf_op jit(solution)/shard_map/while/body/eval_jaxpr/cos | solution.py:79
  72.8 1.3 fusion.58
  74.1 1.3 fusion.59
  76.9 16.5 %fusion.57 = (f32[8192,128]{1,0:T(8,128)S(1)}, f32[8192,128]{1,0:T(8,128)S(1)}) fusion(s32[128]{0:T(128)S(1)} %iota_add_fusion.3), kind=kLoop, calls=%fused_computation.18.clone.1 | loop fusion | flops 15728640 | bytes 8389120 | tf_op jit(solution)/shard_map/while/body/eval_jaxpr/cos | solution.py:79
  93.4 1.3 fusion.58
  94.7 1.3 fusion.59
  97.0 1.2 divide_convert_fusion.1
  98.6 15.9 %all_to_all.30 = bf16[128,2,2,4,128]{4,0,2,1,3:T(8,128)(2,1)} all-to-all(bf16[128,2,2,4,128]{4,0,2,1,3:T(8,128)(2,1)S(1)} %pad_maximum_fusion.2), channel_id=1, replica_groups=mesh['chan'=32,'seg'=4] {'seg'}, dimensions={3} | all-to-all | bytes 1048576 | tf_op jit(solution)/shard_map/all_to_all | solution.py:103
  115.8 186.4 %all-gather.2.cloned.1.call-done = bf16[4096,8,2,128]{3,0,2,1:T(8,128)(2,1)} async-done(((bf16[128,8,2,128]{3,0,2,1:T(8,128)(2,1)}), bf16[4096,8,2,128]{3,0,2,1:T(8,128)(2,1)}) %all-gather.2.cloned.1.call-update) | async-done | bytes 16777232 | tf_op jit(solution)/shard_map/all_gather | solution.py:116
  302.2 18.6 %copy.32 = bf16[4096,8,2,128]{3,1,2,0:T(8,128)(2,1)} copy(bf16[4096,8,2,128]{3,0,2,1:T(8,128)(2,1)} %all-gather.2.cloned.1.call-done) | data formatting | bytes 33554432 | tf_op jit(solution)/shard_map/all_gather | solution.py:116
  320.7 7.9 %gather_fusion = bf16[4,128,8,2,128]{4,2,3,1,0:T(8,128)(2,1)} fusion(bf16[32,128,8,2,128]{4,2,3,1,0:T(8,128)(2,1)} %bitcast.77, s32[1024]{0:T(1024)S(1)} %pad_clamp_fusion), kind=kCustom, calls=%fused_computation | custom fusion | bytes 4194320 | tf_op jit(solution)/shard_map/jit(_take)/gather | solution.py:120
  328.6 4.2 copy.33
  333.3 4.9 fusion.18
  338.2 4.9 fusion.19
  343.1 6.8 %pad_maximum_fusion.1 = bf16[128,2,128,2,128]{0,2,4,1,3:T(8,128)(2,1)} fusion(bf16[128,2,128,1,128]{0,2,4,1,3:T(8,128)(2,1)S(1)} %fusion.19, bf16[128,2,128,1,128]{0,2,4,1,3:T(8,128)(2,1)S(1)} %fusion.18), kind=kLoop, calls=%fused_computation.25 | loop fusion | flops 8388608 | bytes 33554432 | tf_op jit(solution)/shard_map/stack | solution.py:54
  349.9 23.5 %copy.34 = bf16[128,2,128,2,128]{2,4,1,3,0:T(8,128)(2,1)} copy(bf16[128,2,128,2,128]{0,2,4,1,3:T(8,128)(2,1)} %pad_maximum_fusion.1) | data formatting | bytes 33554432 | tf_op jit(solution)/shard_map/stack | solution.py:54
  373.4 12.9 %all-to-all-start.1 = ((bf16[128,2,128,2,128]{2,4,1,3,0:T(8,128)(2,1)}), bf16[128,2,128,2,128]{2,4,1,3,0:T(8,128)(2,1)}, u32[]{:S(2)}, u32[]{:S(2)}) async-start(bf16[128,2,128,2,128]{2,4,1,3,0:T(8,128)(2,1)} %copy.34), calls=%async_computation.1 | async-start | bytes 33554432 | tf_op jit(solution)/shard_map/all_to_all | solution.py:127
  386.3 2.5 cosine_convert_fusion
  388.8 181.2 %all-to-all-done.1 = bf16[128,2,128,2,128]{2,4,1,3,0:T(8,128)(2,1)} async-done(((bf16[128,2,128,2,128]{2,4,1,3,0:T(8,128)(2,1)}), bf16[128,2,128,2,128]{2,4,1,3,0:T(8,128)(2,1)}, u32[]{:S(2)}, u32[]{:S(2)}) %all-to-all-start.1) | async-done | bytes 16777248 | tf_op jit(solution)/shard_map/all_to_all | solution.py:127
  570.0 26.0 %copy.36 = bf16[32,2,128,2,4,128]{5,4,3,2,1,0:T(4,128)(2,1)} copy(bf16[32,2,128,2,4,128]{2,5,1,3,0,4:T(8,128)(2,1)} %bitcast.22) | data formatting | bytes 33554432 | tf_op jit(solution)/shard_map/all_to_all | solution.py:127
  596.0 27.3 %reshape.220 = bf16[8192,1024]{1,0:T(8,128)(2,1)} reshape(bf16[32,2,128,2,4,128]{5,4,3,2,1,0:T(4,128)(2,1)} %copy.36) | data formatting | bytes 33554432 | tf_op jit(solution)/shard_map/reshape | solution.py:58
  623.4 13.7 %convolution_multiply_fusion = f32[8192,256]{1,0:T(8,128)} fusion(bf16[8192,1024]{1,0:T(8,128)(2,1)} %reshape.220, bf16[512,256]{1,0:T(8,128)(2,1)S(1)} %get-tuple-element.99, bf16[512,256]{1,0:T(8,128)(2,1)S(1)} %get-tuple-element.98), kind=kOutput, calls=%fused_computation.28 | convolution fusion | flops 4298113024 | bytes 25690112 | tf_op jit(solution)/shard_map/dot_general | solution.py:59
  (57 shorter events, 4.3 us)
Async XLA Ops:
  6.5 295.6 %all-gather.2.cloned.1.call-start = ((), (), s32[]{:S(2)}) async-start(), calls=%async_computation.2 | async-start | bytes 17301504 | tf_op jit(solution)/shard_map/all_gather | solution.py:116
  15.2 16.5 %copy-start = (bf16[256,8192]{1,0:T(8,128)(2,1)S(1)}, bf16[256,8192]{1,0:T(8,128)(2,1)}, u32[]{:S(2)}) copy-start(bf16[256,8192]{1,0:T(8,128)(2,1)} %get-tuple-element.148) | copy-start | bytes 12582916 | tf_op jit(solution)/shard_map/while
  35.7 16.5 %copy-start = (bf16[256,8192]{1,0:T(8,128)(2,1)S(1)}, bf16[256,8192]{1,0:T(8,128)(2,1)}, u32[]{:S(2)}) copy-start(bf16[256,8192]{1,0:T(8,128)(2,1)} %get-tuple-element.148) | copy-start | bytes 12582916 | tf_op jit(solution)/shard_map/while
  56.3 16.5 %copy-start = (bf16[256,8192]{1,0:T(8,128)(2,1)S(1)}, bf16[256,8192]{1,0:T(8,128)(2,1)}, u32[]{:S(2)}) copy-start(bf16[256,8192]{1,0:T(8,128)(2,1)} %get-tuple-element.148) | copy-start | bytes 12582916 | tf_op jit(solution)/shard_map/while
  76.8 16.5 %copy-start = (bf16[256,8192]{1,0:T(8,128)(2,1)S(1)}, bf16[256,8192]{1,0:T(8,128)(2,1)}, u32[]{:S(2)}) copy-start(bf16[256,8192]{1,0:T(8,128)(2,1)} %get-tuple-element.148) | copy-start | bytes 12582916 | tf_op jit(solution)/shard_map/while
  98.2 16.2 %copy-start.2 = (s32[32]{0:T(128)S(1)}, s32[32]{0:T(128)}, u32[]{:S(2)}) copy-start(s32[32]{0:T(128)} %param.8) | copy-start | bytes 388
  98.2 16.5 %copy-start.1 = (s32[32,16]{0,1:T(8,128)S(1)}, s32[32,16]{0,1:T(8,128)}, u32[]{:S(2)}) copy-start(s32[32,16]{0,1:T(8,128)} %param.7) | copy-start | bytes 6148
  98.3 16.9 %copy-start.3 = (s32[64]{0:T(128)S(1)}, s32[64]{0:T(128)}, u32[]{:S(2)}) copy-start(s32[64]{0:T(128)} %param.9) | copy-start | bytes 772
  373.4 196.6 %all-to-all-start.1 = ((bf16[128,2,128,2,128]{2,4,1,3,0:T(8,128)(2,1)}), bf16[128,2,128,2,128]{2,4,1,3,0:T(8,128)(2,1)}, u32[]{:S(2)}, u32[]{:S(2)}) async-start(bf16[128,2,128,2,128]{2,4,1,3,0:T(8,128)(2,1)} %copy.34), calls=%async_computation.1 | async-start | bytes 33554432 | tf_op jit(solution)/shard_map/all_to_all | solution.py:127
Sparse Core Ops, SparseCore 0:
  114.6 187.5 all-gather.1
where the time goes:
time: 647 us; the launch traced here: 644 us
  waiting for transfers between devices  368 us (57%)
  local copies, waits for them, and re-layouts  119 us (18%)
  other arithmetic  76.8 us (12%)
  matrix products  35.1 us (5%)
  blocking collectives  15.9 us (2%)
  between operations  13.6 us (2%)
  starting transfers between devices  12.9 us (2%)
    all_gather x1, waiting for transfers between devices, on_device(): incoming = lax.all_gather(quarter, 'chan', axis=0, tiled=True)  186 us
    all_to_all x1, waiting for transfers between devices, on_device(): lax.all_to_all(spectra, 'seg', split_axis=0, concat_axis=4, tiled=True)  181 us
    cos x4, other arithmetic, transform(): table_part = jnp.concatenate([jnp.cos(angles), -jnp.sin(angles)], axis=1)  66.1 us
    reshape x1, local copies, waits for them, and re-layouts, invert(): flat = spectra.reshape(-1, spectra.shape[3] * spectra.shape[4])  27.3 us
    all_to_all x1, local copies, waits for them, and re-layouts, on_device(): lax.all_to_all(spectra, 'seg', split_axis=0, concat_axis=4, tiled=True)  26 us
    another operation x1, local copies, waits for them, and re-layouts, cross_terms(): return jnp.stack([real_part, imag_part], axis=3).astype(jnp.bfloat16)  23.5 us
    all_gather x1, local copies, waits for them, and re-layouts, on_device(): incoming = lax.all_gather(quarter, 'chan', axis=0, tiled=True)  18.6 us
    all_to_all x1, blocking collectives, on_device(): lax.all_to_all(whitened, 'seg', split_axis=3, concat_axis=1, tiled=True)  15.9 us
  transfers between devices with their start and end apart: 2, of which 2 were waited for; matrix products, arithmetic and copies ran while one was open for 1% of the time, Pallas kernels for 0%

commit v1 on v0

--- a/solution.py
+++ b/solution.py
@@ -113,7 +113,9 @@
         ]
     )
     empty_blocks = jnp.zeros((2 * TILE_DEV, block_size, all_segs, 2, quarter_bins), jnp.bfloat16)
-    incoming = lax.all_gather(quarter, "chan", axis=0, tiled=True)
+    incoming = jnp.concatenate(
+        lax.all_to_all(jnp.stack([quarter] * lax.axis_size("chan")), "chan", 0, 0), axis=0
+    )
     block_total = incoming.shape[0] // block_size
     incoming_blocks = incoming.reshape(block_total, block_size, all_segs, 2, quarter_bins)
     inside = (needed >= 0) & (needed < block_total)

time: 647 us -> 730 us (1.13)
  the two profiles are of different devices: /device:TPU:1 before, /device:TPU:2 now
where the time goes in v1:
time: 730 us; the launch traced here: 727 us
  waiting for transfers between devices  469 us (64%)
  local copies, waits for them, and re-layouts  107 us (15%)
  other arithmetic  76.8 us (11%)
  matrix products  35.1 us (5%)
  starting transfers between devices  20.7 us (3%)
  blocking collectives  15.3 us (2%)
    all_to_all x1, waiting for transfers between devices, on_device(): lax.all_to_all(jnp.stack([quarter] * lax.axis_size('chan')), 'chan', 0, 0)  286 us
    all_to_all x1, waiting for transfers between devices, on_device(): lax.all_to_all(spectra, 'seg', split_axis=0, concat_axis=4, tiled=True)  183 us
    cos x4, other arithmetic, transform(): table_part = jnp.concatenate([jnp.cos(angles), -jnp.sin(angles)], axis=1)  66.1 us
    reshape x1, local copies, waits for them, and re-layouts, invert(): flat = spectra.reshape(-1, spectra.shape[3] * spectra.shape[4])  27.3 us
    all_to_all x1, local copies, waits for them, and re-layouts, on_device(): lax.all_to_all(spectra, 'seg', split_axis=0, concat_axis=4, tiled=True)  26 us
    another operation x1, local copies, waits for them, and re-layouts, cross_terms(): return jnp.stack([real_part, imag_part], axis=3).astype(jnp.bfloat16)  23.5 us
    all_to_all x1, blocking collectives, on_device(): lax.all_to_all(whitened, 'seg', split_axis=3, concat_axis=1, tiled=True)  15.3 us
  transfers between devices with their start and end apart: 2, of which 2 were waited for; matrix products, arithmetic and copies ran while one was open for 1% of the time, Pallas kernels for 0%

profile of v1, /device:TPU:2, one launch (start us, length us, event | category | flops | bytes accessed | tf_op | source)
XLA Modules:
  0.0 727.0 jit_solution(270946525019661823)
XLA Ops:
  0.1 7.2 reshape.211
  7.3 82.4 %while.13 = (s32[]{:T(128)}, f32[4,256,256]{1,2,0:T(8,128)S(1)}, s32[4]{0:T(128)S(1)}, bf16[256,8192]{1,0:T(8,128)(2,1)}, s32[]{:T(128)}, /*index=5*/s32[1]{0:T(128)}, s32[1]{0:T(128)}) while((s32[]{:T(128)}, f32[4,256,256]{1,2,0:T(8,128)S(1)}, s32[4]{0:T(128)S(1)}, bf16[256,8192]{1,0:T(8,128)(2,1)}, s32[]{:T(128)}, ...), condition=%wide.region_8.9_spmd.clone, body=%wide.region_7.8_spmd.clone.sunk | while | flops 2182152192 | bytes 51119260 | solution.py:85
  8.7 16.5 %fusion.57 = (f32[8192,128]{1,0:T(8,128)S(1)}, f32[8192,128]{1,0:T(8,128)S(1)}) fusion(s32[128]{0:T(128)S(1)} %iota_add_fusion.3), kind=kLoop, calls=%fused_computation.18.clone.1 | loop fusion | flops 15728640 | bytes 8389120 | tf_op jit(solution)/shard_map/while/body/eval_jaxpr/cos | solution.py:79
  25.2 1.3 fusion.58
  26.5 1.3 fusion.59
  29.2 16.5 %fusion.57 = (f32[8192,128]{1,0:T(8,128)S(1)}, f32[8192,128]{1,0:T(8,128)S(1)}) fusion(s32[128]{0:T(128)S(1)} %iota_add_fusion.3), kind=kLoop, calls=%fused_computation.18.clone.1 | loop fusion | flops 15728640 | bytes 8389120 | tf_op jit(solution)/shard_map/while/body/eval_jaxpr/cos | solution.py:79
  45.7 1.3 fusion.58
  47.0 1.3 fusion.59
  48.4 0.7 dynamic_slice.19
  49.8 16.5 %fusion.57 = (f32[8192,128]{1,0:T(8,128)S(1)}, f32[8192,128]{1,0:T(8,128)S(1)}) fusion(s32[128]{0:T(128)S(1)} %iota_add_fusion.3), kind=kLoop, calls=%fused_computation.18.clone.1 | loop fusion | flops 15728640 | bytes 8389120 | tf_op jit(solution)/shard_map/while/body/eval_jaxpr/cos | solution.py:79
  66.3 1.3 fusion.58
  67.6 1.3 fusion.59
  70.3 16.5 %fusion.57 = (f32[8192,128]{1,0:T(8,128)S(1)}, f32[8192,128]{1,0:T(8,128)S(1)}) fusion(s32[128]{0:T(128)S(1)} %iota_add_fusion.3), kind=kLoop, calls=%fused_computation.18.clone.1 | loop fusion | flops 15728640 | bytes 8389120 | tf_op jit(solution)/shard_map/while/body/eval_jaxpr/cos | solution.py:79
  86.8 1.3 fusion.58
  88.2 1.3 fusion.59
  90.5 1.2 divide_convert_fusion.1
  92.0 15.3 %all_to_all.35 = bf16[128,2,2,4,128]{4,0,2,1,3:T(8,128)(2,1)S(1)} all-to-all(bf16[128,2,2,4,128]{4,0,2,1,3:T(8,128)(2,1)S(1)} %pad_maximum_fusion.2), channel_id=1, replica_groups=mesh['chan'=32,'seg'=4] {'seg'}, dimensions={3} | all-to-all | bytes 1048576 | tf_op jit(solution)/shard_map/all_to_all | solution.py:103
  107.6 6.2 stack.31
  113.8 8.3 %all-to-all-start.1 = ((bf16[32,128,8,2,128]{4,2,3,1,0:T(8,128)(2,1)}), bf16[32,128,8,2,128]{4,2,3,1,0:T(8,128)(2,1)}, u32[]{:S(2)}, u32[]{:S(2)}) async-start(bf16[32,128,8,2,128]{4,2,3,1,0:T(8,128)(2,1)} %stack.31), calls=%async_computation.1 | async-start | bytes 33554432 | tf_op jit(solution)/shard_map/all_to_all | solution.py:117
  123.5 285.8 %all-to-all-done.1 = bf16[32,128,8,2,128]{4,2,3,1,0:T(8,128)(2,1)} async-done(((bf16[32,128,8,2,128]{4,2,3,1,0:T(8,128)(2,1)}), bf16[32,128,8,2,128]{4,2,3,1,0:T(8,128)(2,1)}, u32[]{:S(2)}, u32[]{:S(2)}) %all-to-all-start.1) | async-done | bytes 16777248 | tf_op jit(solution)/shard_map/all_to_all | solution.py:117
  409.3 7.9 %gather_fusion = bf16[4,128,8,2,128]{4,2,3,1,0:T(8,128)(2,1)} fusion(bf16[32,128,8,2,128]{4,2,3,1,0:T(8,128)(2,1)} %all-to-all-done.1, s32[1024]{0:T(1024)S(1)} %pad_clamp_fusion), kind=kCustom, calls=%fused_computation | custom fusion | bytes 4194320 | tf_op jit(solution)/shard_map/jit(_take)/gather | solution.py:122
  417.2 4.2 copy.33
  421.9 4.9 fusion.18
  426.8 4.9 fusion.19
  431.6 6.8 pad_maximum_fusion.1
  438.4 23.5 %copy.34 = bf16[128,2,128,2,128]{2,4,1,3,0:T(8,128)(2,1)} copy(bf16[128,2,128,2,128]{0,2,4,1,3:T(8,128)(2,1)} %pad_maximum_fusion.1) | data formatting | bytes 33554432 | tf_op jit(solution)/shard_map/stack | solution.py:54
  461.9 12.4 %all-to-all-start.2 = ((bf16[128,2,128,2,128]{2,4,1,3,0:T(8,128)(2,1)}), bf16[128,2,128,2,128]{2,4,1,3,0:T(8,128)(2,1)}, u32[]{:S(2)}, u32[]{:S(2)}) async-start(bf16[128,2,128,2,128]{2,4,1,3,0:T(8,128)(2,1)} %copy.34), calls=%async_computation.2 | async-start | bytes 33554432 | tf_op jit(solution)/shard_map/all_to_all | solution.py:129
  474.4 2.5 cosine_convert_fusion
  476.9 183.0 %all-to-all-done.2 = bf16[128,2,128,2,128]{2,4,1,3,0:T(8,128)(2,1)} async-done(((bf16[128,2,128,2,128]{2,4,1,3,0:T(8,128)(2,1)}), bf16[128,2,128,2,128]{2,4,1,3,0:T(8,128)(2,1)}, u32[]{:S(2)}, u32[]{:S(2)}) %all-to-all-start.2) | async-done | bytes 16777248 | tf_op jit(solution)/shard_map/all_to_all | solution.py:129
  659.9 26.0 %copy.36 = bf16[32,2,128,2,4,128]{5,4,3,2,1,0:T(4,128)(2,1)} copy(bf16[32,2,128,2,4,128]{2,5,1,3,0,4:T(8,128)(2,1)} %bitcast.21) | data formatting | bytes 33554432 | tf_op jit(solution)/shard_map/all_to_all | solution.py:129
  686.0 27.3 %reshape.214 = bf16[8192,1024]{1,0:T(8,128)(2,1)} reshape(bf16[32,2,128,2,4,128]{5,4,3,2,1,0:T(4,128)(2,1)} %copy.36) | data formatting | bytes 33554432 | tf_op jit(solution)/shard_map/reshape | solution.py:58
  713.3 13.7 %convolution_multiply_fusion = f32[8192,256]{1,0:T(8,128)} fusion(bf16[8192,1024]{1,0:T(8,128)(2,1)} %reshape.214, bf16[512,256]{1,0:T(8,128)(2,1)S(1)} %get-tuple-element.99, bf16[512,256]{1,0:T(8,128)(2,1)S(1)} %get-tuple-element.98), kind=kOutput, calls=%fused_computation.28 | convolution fusion | flops 4298113024 | bytes 25690112 | tf_op jit(solution)/shard_map/dot_general | solution.py:59
  (57 shorter events, 5.3 us)
Async XLA Ops:
  8.6 16.5 %copy-start = (bf16[256,8192]{1,0:T(8,128)(2,1)S(1)}, bf16[256,8192]{1,0:T(8,128)(2,1)}, u32[]{:S(2)}) copy-start(bf16[256,8192]{1,0:T(8,128)(2,1)} %get-tuple-element.148) | copy-start | bytes 12582916 | tf_op jit(solution)/shard_map/while
  29.2 16.5 %copy-start = (bf16[256,8192]{1,0:T(8,128)(2,1)S(1)}, bf16[256,8192]{1,0:T(8,128)(2,1)}, u32[]{:S(2)}) copy-start(bf16[256,8192]{1,0:T(8,128)(2,1)} %get-tuple-element.148) | copy-start | bytes 12582916 | tf_op jit(solution)/shard_map/while
  49.7 16.5 %copy-start = (bf16[256,8192]{1,0:T(8,128)(2,1)S(1)}, bf16[256,8192]{1,0:T(8,128)(2,1)}, u32[]{:S(2)}) copy-start(bf16[256,8192]{1,0:T(8,128)(2,1)} %get-tuple-element.148) | copy-start | bytes 12582916 | tf_op jit(solution)/shard_map/while
  70.3 16.5 %copy-start = (bf16[256,8192]{1,0:T(8,128)(2,1)S(1)}, bf16[256,8192]{1,0:T(8,128)(2,1)}, u32[]{:S(2)}) copy-start(bf16[256,8192]{1,0:T(8,128)(2,1)} %get-tuple-element.148) | copy-start | bytes 12582916 | tf_op jit(solution)/shard_map/while
  113.8 8.3 %copy-start.2 = (s32[32]{0:T(128)S(1)}, s32[32]{0:T(128)}, u32[]{:S(2)}) copy-start(s32[32]{0:T(128)} %param.8) | copy-start | bytes 388
  113.8 8.6 %copy-start.1 = (s32[32,16]{0,1:T(8,128)S(1)}, s32[32,16]{0,1:T(8,128)}, u32[]{:S(2)}) copy-start(s32[32,16]{0,1:T(8,128)} %param.7) | copy-start | bytes 6148
  113.8 9.0 %copy-start.3 = (s32[64]{0:T(128)S(1)}, s32[64]{0:T(128)}, u32[]{:S(2)}) copy-start(s32[64]{0:T(128)} %param.9) | copy-start | bytes 772
  113.8 295.5 %all-to-all-start.1 = ((bf16[32,128,8,2,128]{4,2,3,1,0:T(8,128)(2,1)}), bf16[32,128,8,2,128]{4,2,3,1,0:T(8,128)(2,1)}, u32[]{:S(2)}, u32[]{:S(2)}) async-start(bf16[32,128,8,2,128]{4,2,3,1,0:T(8,128)(2,1)} %stack.31), calls=%async_computation.1 | async-start | bytes 33554432 | tf_op jit(solution)/shard_map/all_to_all | solution.py:117
  461.9 198.0 %all-to-all-start.2 = ((bf16[128,2,128,2,128]{2,4,1,3,0:T(8,128)(2,1)}), bf16[128,2,128,2,128]{2,4,1,3,0:T(8,128)(2,1)}, u32[]{:S(2)}, u32[]{:S(2)}) async-start(bf16[128,2,128,2,128]{2,4,1,3,0:T(8,128)(2,1)} %copy.34), calls=%async_computation.2 | async-start | bytes 33554432 | tf_op jit(solution)/shard_map/all_to_all | solution.py:129
